TPU v7x, 256 devices: a whole 4x4x8 slice. The times are simulated.
256 devices in a mesh: row: 32 (over y, z), col: 8 (over x, core).
Axes of the slice: x: 4, y: 4, z: 8, core: 2. Of those that a mesh axis runs over, the one named last changes fastest.
Arguments:
- query_acts: bfloat16 [256, 8192], P('col', 'row'), may hold values from -6 to 6
- query_grads: bfloat16 [256, 28672], P('row', 'col'), may hold values from -6 to 6
- ritz_mats: float32 [3, 8192, 28672], P(None, 'row', 'col'), may hold values from -0.095683193 to 0.095683193, as said below
- eigenvalues: float32 [3], replicated, may hold values from 0.5 to 4
- train_acts: bfloat16 [256, 8192], P('row'), may hold values from -6 to 6
- train_grads: bfloat16 [256, 28672], P('row', 'col'), may hold values from -6 to 6
Outputs:
- response: bfloat16 [256, 28672], P('row', 'col')
- scores: float32 [256], P('row')
Inputs may be any that keep to these rules, and one draw needn't show every extreme that they name: `ritz_mats`: real entries of order one over the square root of 8192; every matrix has full rank.
All inputs are finite; a program needn't handle non-finite values.
Results may differ from a plain program's by a relative error of at most 0.0012.
Values may be sent and summed in bfloat16 or wider, within the bound.
A program may use at most 64 MiB of HBM per device.

v0:
```python
import math

import jax
import jax.numpy as jnp
from jax import lax
from jax.sharding import PartitionSpec as P

D_OUT = 28672
QUERY = 256


highest = lax.Precision.HIGHEST


def per_device(query_acts, query_grads, ritz_mats, eigenvalues, train_acts, train_grads):
    acts_all = lax.all_gather(query_acts, "col", axis=0, tiled=True)
    grad_tile = lax.dot_general(
        acts_all,
        lax.all_gather(query_grads, "row", axis=0, tiled=True),
        (((0,), (0,)), ((), ())),
        preferred_element_type=jnp.float32,
    )
    local_terms = jnp.sum(ritz_mats * grad_tile[None], axis=(1, 2))
    coeffs = lax.psum(local_terms, ("row", "col"))
    weights = coeffs / (eigenvalues * math.sqrt(QUERY * D_OUT))
    train_local = lax.all_to_all(train_acts, "row", split_axis=1, concat_axis=0, tiled=True).astype(
        jnp.float32
    )
    combined = jnp.tensordot(weights, ritz_mats, axes=1, precision=highest)
    root_width = math.sqrt(D_OUT)
    response_full = lax.psum_scatter(
        jnp.dot(train_local, combined, precision=highest), "row", scatter_dimension=0, tiled=True
    )
    score_terms = jnp.sum(response_full * train_grads.astype(jnp.float32), axis=1) / root_width
    scores = lax.psum(score_terms, "col")
    response = response_full.astype(jnp.bfloat16)
    return (response, scores)


def solution(mesh):
    in_specs = (
        P("col", "row"),
        P("row", "col"),
        P(None, "row", "col"),
        P(),
        P("row", None),
        P("row", "col"),
    )
    out_specs = (P("row", "col"), P("row"))
    return jax.shard_map(
        per_device, mesh=mesh, in_specs=in_specs, out_specs=out_specs, check_vma=False
    )
```

profile of v0, /device:TPU:1, one launch (start us, length us, event | category | flops | bytes accessed | tf_op | source)
XLA Modules:
  0.0 477.4 jit_solution(8239477549064250648)
XLA Ops:
  7.2 0.0 all-gather.2.cloned.1.call-start
  7.2 0.7 all-gather.2.cloned.1.call-update
  7.9 16.0 %all_gather.6 = bf16[256,256]{1,0:T(8,128)(2,1)S(1)} all-gather(bf16[32,256]{1,0:T(8,128)(2,1)} %param.6), channel_id=1, replica_groups=mesh['row'=32,'col'=8] {'col'}, dimensions={0}, use_global_device_ids=true | all-gather | bytes 147456 | tf_op jit(solution)/shard_map/all_gather | solution.py:16
  23.9 64.0 %all-gather.2.cloned.1.call-done = bf16[256,3584]{1,0:T(8,128)(2,1)} async-done(((bf16[8,3584]{1,0:T(8,128)(2,1)}), bf16[256,3584]{1,0:T(8,128)(2,1)}) %all-gather.2.cloned.1.call-update) | async-done | bytes 1835024 | tf_op jit(solution)/shard_map/all_gather | solution.py:19
  87.9 2.2 fusion.8
  90.1 0.0 copy-start.1
  90.1 5.3 %multiply_reduce_fusion = f32[3]{0:T(128)S(1)} fusion(f32[3,256,3584]{2,1,0:T(8,128)} %param.8, f32[256,3584]{1,0:T(8,128)S(1)} %fusion.8), kind=kLoop, calls=%fused_computation.2 | loop fusion | flops 5505021 | bytes 14680076 | tf_op jit(solution)/shard_map/reduce_sum | solution.py:23
  95.4 5.3 %all-to-all-start = ((bf16[8,32,256]{2,0,1:T(8,128)(2,1)}), bf16[8,32,256]{2,0,1:T(8,128)(2,1)S(1)}, u32[]{:S(2)}, u32[]{:S(2)}) async-start(bf16[8,32,256]{2,0,1:T(8,128)(2,1)} %bitcast.2), calls=%async_computation | async-start | bytes 262144 | tf_op jit(solution)/shard_map/all_to_all | solution.py:26
  100.7 0.0 reduce-scatter.4.cloned.1.call-start
  100.8 80.7 %psum.14 = f32[3]{0:T(128)S(1)} all-reduce(f32[3]{0:T(128)S(1)} %multiply_reduce_fusion), channel_id=1, replica_groups=mesh['row'=32,'col'=8] {'row','col'}, use_global_device_ids=true, to_apply=%region_1.0 | all-reduce | flops 3 | bytes 24 | tf_op jit(solution)/shard_map/psum | solution.py:24
  181.5 0.0 copy-done.1
  181.5 40.2 %fusion = f32[1,256,3584]{2,0,1:T(1,128)} fusion(f32[3,256,3584]{2,1,0:T(8,128)} %param.8, f32[3]{0:T(128)S(1)} %psum.14, f32[3]{0:T(128)S(1)} %copy-done.1), kind=kOutput, calls=%fused_computation | convolution fusion | flops 33030150 | bytes 14680088 | tf_op jit(solution)/shard_map/dot_general | solution.py:29
  221.7 0.0 all-to-all-done
  221.7 6.9 %convolution_bitcast_fusion = f32[256,3584]{0,1:T(8,128)} fusion(f32[1,256,3584]{2,0,1:T(1,128)} %fusion, bf16[8,32,256]{2,0,1:T(8,128)(2,1)S(1)} %all-to-all-done), kind=kOutput, calls=%fused_computation.3 | convolution fusion | flops 2818572288 | bytes 7471104 | tf_op jit(solution)/shard_map/dot_general | solution.py:32
  228.6 5.2 %copy.14 = f32[256,3584]{1,0:T(8,128)} copy(f32[256,3584]{0,1:T(8,128)} %convolution_bitcast_fusion) | data formatting | bytes 7340032
  233.7 0.0 copy-start
  233.7 0.0 reduce-scatter.4.cloned.1.call-update
  233.8 0.8 copy-done
  234.6 0.3 copy.10
  234.9 211.5 %reduce-scatter.4.cloned.1.call-done = f32[8,3584]{1,0:T(8,128)} async-done(((f32[256,3584]{1,0:T(8,128)}), f32[8,3584]{1,0:T(8,128)}) %reduce-scatter.4.cloned.1.call-update) | async-done | bytes 114704
  446.4 2.7 copy.15
  449.1 2.5 multiply_reduce_fusion.1
  451.6 0.9 copy.11
  452.5 18.1 %psum.15 = f32[8]{0:T(128)} all-reduce(f32[8]{0:T(128)S(1)} %broadcast_multiply_fusion), channel_id=1, replica_groups=mesh['row'=32,'col'=8] {'col'}, use_global_device_ids=true, to_apply=%region_4.0 | all-reduce | flops 8 | bytes 64 | tf_op jit(solution)/shard_map/psum | solution.py:35
  (1 shorter events, 0.0 us)
Async XLA Ops:
  7.2 80.8 %all-gather.2.cloned.1.call-start = ((), (), s32[]{:S(2)}) async-start(), calls=%async_computation.2 | async-start | bytes 1892352 | tf_op jit(solution)/shard_map/all_gather | solution.py:19
  90.1 91.4 %copy-start.1 = (f32[3]{0:T(128)S(1)}, f32[3]{0:T(128)}, u32[]{:S(2)}) copy-start(f32[3]{0:T(128)} %param.9) | copy-start | bytes 40
  95.4 126.3 %all-to-all-start = ((bf16[8,32,256]{2,0,1:T(8,128)(2,1)}), bf16[8,32,256]{2,0,1:T(8,128)(2,1)S(1)}, u32[]{:S(2)}, u32[]{:S(2)}) async-start(bf16[8,32,256]{2,0,1:T(8,128)(2,1)} %bitcast.2), calls=%async_computation | async-start | bytes 262144 | tf_op jit(solution)/shard_map/all_to_all | solution.py:26
  100.7 345.7 %reduce-scatter.4.cloned.1.call-start = ((), (), s32[]{:S(2)}) async-start(), calls=%async_computation.3 | async-start | bytes 3784704
  233.7 0.8 copy-start
Sparse Core Ops, SparseCore 0:
  10.6 77.3 all-gather.1
  233.9 212.4 reduce-scatter.3
where the time goes:
time: 478 us; the launch traced here: 477 us
  waiting for transfers between devices  276 us (58%)
  blocking collectives  115 us (24%)
  matrix products  49.2 us (10%)
  between operations  14.1 us (3%)
  local copies, waits for them, and re-layouts  9.87 us (2%)
  other arithmetic  7.81 us (2%)
  starting transfers between devices  5.4 us (1%)
    unnamed x3, waiting for transfers between devices  212 us
    psum x1, blocking collectives, per_device(): coeffs = lax.psum(local_terms, ('row', 'col'))  80.7 us
    all_gather x1, waiting for transfers between devices, per_device(): lax.all_gather(query_grads, 'row', axis=0, tiled=True)  64 us
    dot_general x1, matrix products, per_device(): combined = jnp.tensordot(weights, ritz_mats, axes=1, precision=highest)  40.2 us
    psum x1, blocking collectives, per_device(): scores = lax.psum(score_terms, 'col')  18.1 us
    all_gather x1, blocking collectives, per_device(): acts_all = lax.all_gather(query_acts, 'col', axis=0, tiled=True)  16 us
    unnamed x7, local copies, waits for them, and re-layouts  9.57 us
  transfers between devices with their start and end apart: 3, of which 2 were waited for; matrix products, arithmetic and copies ran while one was open for 8% of the time, Pallas kernels for 0%

commit v1 on v0

v1 whole, which is shorter than its diff:
```python
import math

import jax
import jax.numpy as jnp
from jax import lax
from jax.experimental import pallas as pl
from jax.experimental.pallas import tpu as pltpu
from jax.sharding import PartitionSpec as P

MESH = pl.DeviceIdType.MESH
F32, BF16 = jnp.float32, jnp.bfloat16

D_OUT = 28672
QUERY = 256
NY, NZ = 4, 8
ROWS = NY * NZ
COLS = 8
RITZ = 3
TOK = 256
OWN = TOK // ROWS
FEAT = 8192 // ROWS
WIDTH = D_OUT // COLS
CHUNK = 512
TILE = 256

GZ = 2048
GY = WIDTH - GZ
SZ = 1536
SY = WIDTH - SZ


class Wire:
    def __init__(self, send_sem, recv_sem):
        self.send_sem, self.recv_sem = send_sem, recv_sem
        self.used = 0
        self.sent = []

    def put(self, src, dst, land, device):
        i = self.used
        self.used += 1
        pair = dict(send_sem=self.send_sem.at[i], recv_sem=self.recv_sem.at[i], device_id=device, device_id_type=MESH)
        copy = pltpu.make_async_remote_copy(src_ref=src, dst_ref=dst, **pair)
        copy.start()
        self.sent.append(copy)
        return pltpu.make_async_remote_copy(src_ref=land, dst_ref=land, **pair)

    def drain(self):
        for copy in self.sent:
            copy.wait_send()


N_WIRE = 96


def kernel(
    qa, qg, ritz, eig, ta, tg,
    response, scores,
    r_buf, hl, up, a_all, t_all, g_z, g_y, tg_buf,
    z1_send, z1_recv, y1_send, y1_recv, z2, y2, z2_send, z2_recv, y2_send, y2_recv,
    c_col, c_row, s_col,
    load_sem, wire_send, wire_recv, all_send, all_recv,
):
    row, col = lax.axis_index("row"), lax.axis_index("col")
    y, z = row // NZ, lax.rem(row, NZ)

    def at_z(step):
        return lax.rem(z + (step + NZ), NZ)

    def at_y(step):
        return lax.rem(y + (step + NY), NY)

    def z_dev(step):
        return {"row": y * NZ + at_z(step)}

    def y_dev(step):
        return {"row": at_y(step) * NZ + z}

    loads = [
        pltpu.make_async_copy(qa, a_all.at[col], load_sem.at[0]),
        pltpu.make_async_copy(qg.at[:, pl.ds(0, GZ)], g_z.at[y, 0], load_sem.at[1]),
        pltpu.make_async_copy(qg.at[:, pl.ds(GZ, GY)], g_y.at[0, z], load_sem.at[2]),
        pltpu.make_async_copy(
            ta.at[:, pl.ds(pl.multiple_of(row * FEAT, FEAT), FEAT)], t_all.at[row], load_sem.at[3]
        ),
        pltpu.make_async_copy(tg, tg_buf, load_sem.at[4]),
    ]
    n_small = len(loads)
    for c in range(WIDTH // CHUNK):
        part = pl.ds(c * CHUNK, CHUNK)
        loads.append(
            pltpu.make_async_copy(ritz.at[:, :, part], r_buf.at[:, :, part], load_sem.at[n_small + c])
        )
    for load in loads:
        load.start()

    barrier = pltpu.get_barrier_semaphore()

    @pl.loop(1, ROWS)
    def _(d):
        pl.semaphore_signal(
            barrier, inc=1, device_id={"row": lax.rem(row + d, ROWS)}, device_id_type=MESH
        )

    @pl.loop(1, COLS)
    def _(d):
        pl.semaphore_signal(
            barrier, inc=1, device_id={"col": lax.rem(col + d, COLS)}, device_id_type=MESH
        )

    pl.semaphore_wait(barrier, ROWS - 1 + COLS - 1)

    wire = Wire(wire_send, wire_recv)

    def spread(src, dst, i, axis, count):
        me = lax.axis_index(axis)

        @pl.loop(1, count)
        def _(d):
            pltpu.make_async_remote_copy(
                src_ref=src, dst_ref=dst, send_sem=all_send.at[i], recv_sem=all_recv.at[i],
                device_id={axis: lax.rem(me + d, count)}, device_id_type=MESH,
            ).start()

    def spread_done(buf, i, axis, count):
        whole = buf.at[pl.ds(0, count - 1)]
        return pltpu.make_async_remote_copy(
            src_ref=whole, dst_ref=whole, send_sem=all_send.at[i], recv_sem=all_recv.at[i],
            device_id={axis: 0}, device_id_type=MESH,
        )

    first, second = pl.ds(0, GZ // 2), pl.ds(GZ // 2, GZ // 2)
    y_first, y_second = pl.ds(0, GY // 2), pl.ds(GY // 2, GY // 2)

    def zz(hop):
        if hop < 3:
            src_r, dst_r = max(2 * hop - 1, 0), 2 * hop + 1
            src_l, dst_l = 2 * hop, 2 * hop + 2
            own = qg.at[:, pl.ds(0, GZ)]
            return (
                wire.put(own if hop == 0 else g_z.at[y, src_r], g_z.at[y, dst_r], g_z.at[y, dst_r], z_dev(1)),
                wire.put(own if hop == 0 else g_z.at[y, src_l], g_z.at[y, dst_l], g_z.at[y, dst_l], z_dev(-1)),
            )
        return (
            wire.put(g_z.at[y, 5, :, first], g_z.at[y, 7, :, first], g_z.at[y, 7, :, first], z_dev(1)),
            wire.put(g_z.at[y, 6, :, second], g_z.at[y, 7, :, second], g_z.at[y, 7, :, second], z_dev(-1)),
        )

    def zy(lo, hi):
        slots = pl.ds(lo, hi - lo)
        src = g_z.at[y, slots]
        return (
            wire.put(src, g_z.at[y, slots], g_z.at[at_y(-1), slots], y_dev(1)),
            wire.put(src, g_z.at[y, slots], g_z.at[at_y(1), slots], y_dev(-1)),
        )

    def zy_on(lo, hi):
        slots = pl.ds(lo, hi - lo)
        across = at_y(2)
        return (
            wire.put(
                g_z.at[at_y(-1), slots, :, first], g_z.at[at_y(-1), slots, :, first],
                g_z.at[across, slots, :, first], y_dev(1),
            ),
            wire.put(
                g_z.at[at_y(1), slots, :, second], g_z.at[at_y(1), slots, :, second],
                g_z.at[across, slots, :, second], y_dev(-1),
            ),
        )

    def yy(hop):
        if hop == 0:
            own = qg.at[:, pl.ds(GZ, GY)]
            return (
                wire.put(own, g_y.at[1, z], g_y.at[1, z], y_dev(1)),
                wire.put(own, g_y.at[2, z], g_y.at[2, z], y_dev(-1)),
            )
        return (
            wire.put(g_y.at[1, z, :, y_first], g_y.at[3, z, :, y_first], g_y.at[3, z, :, y_first], y_dev(1)),
            wire.put(g_y.at[2, z, :, y_second], g_y.at[3, z, :, y_second], g_y.at[3, z, :, y_second], y_dev(-1)),
        )

    def yz(lo, hi, hop):
        slots = pl.ds(lo, hi - lo)
        right = g_y.at[slots, at_z(-hop)] if hop < 3 else g_y.at[slots, at_z(-hop), :, y_first]
        left = g_y.at[slots, at_z(hop)] if hop < 3 else g_y.at[slots, at_z(hop), :, y_second]
        land_r = g_y.at[slots, at_z(-hop - 1)] if hop < 3 else g_y.at[slots, at_z(-hop - 1), :, y_first]
        land_l = g_y.at[slots, at_z(hop + 1)] if hop < 3 else g_y.at[slots, at_z(hop + 1), :, y_second]
        return (wire.put(right, right, land_r, z_dev(1)), wire.put(left, left, land_l, z_dev(-1)))

    def arrived(copies):
        for copy in copies:
            copy.wait_recv()

    def product(c, lhs, split):
        if split:
            loads[n_small + c].wait()

        @pl.loop(0, RITZ * (CHUNK // TILE))
        def _(i):
            k = i // (CHUNK // TILE)
            part = pl.ds(pl.multiple_of(c * CHUNK + lax.rem(i, CHUNK // TILE) * TILE, TILE), TILE)
            if split:
                entry = r_buf[k, :, part]
                high = entry.astype(BF16)
                low = (entry - high.astype(F32)).astype(BF16)
                hl[k, 0, :, part] = high
                hl[k, 1, :, part] = low
            else:
                high, low = hl[k, 0, :, part], hl[k, 1, :, part]
            acts = lhs[...].reshape(TOK, FEAT)
            out = jnp.dot(acts, high, preferred_element_type=F32) + jnp.dot(
                acts, low, preferred_element_type=F32
            )
            up[k, :, :, :, part] = out.reshape(NY, NZ, OWN, TILE)

    zz0 = zz(0)
    yy0 = yy(0)
    spread(qa, a_all.at[col], 0, "col", COLS)
    for load in loads[:n_small]:
        load.wait()
    zy0 = zy(0, 1)
    yz0 = yz(0, 1, 0)
    arrived(zz0)
    zz1, zy1 = zz(1), zy(1, 3)
    arrived(yy0)
    yy1 = yy(1)
    arrived(yz0)
    yz0 = yz(0, 1, 1)
    spread_done(a_all, 0, "col", COLS).wait_recv()
    product(0, a_all, True)

    arrived(zz1)
    zz2, zy2 = zz(2), zy(3, 5)
    arrived(zy0)
    zo0 = zy_on(0, 1)
    arrived(yy1)
    yg0 = yz(1, 4, 0)
    arrived(yz0)
    yz0 = yz(0, 1, 2)
    product(1, a_all, True)

    arrived(zz2)
    zz3 = zz(3)
    arrived(zy1)
    zo1 = zy_on(1, 3)
    arrived(yz0)
    yz0 = yz(0, 1, 3)
    arrived(yg0)
    yg0 = yz(1, 4, 1)
    product(2, a_all, True)

    arrived(zz3)
    zy3 = zy(5, 8)
    arrived(zy2)
    zo2 = zy_on(3, 5)
    product(3, a_all, True)
    arrived(yg0)
    yg0 = yz(1, 4, 2)
    product(4, a_all, True)
    arrived(zy3)
    zo3 = zy_on(5, 8)
    arrived(yg0)
    yg0 = yz(1, 4, 3)

    @pl.loop(1, ROWS)
    def _(d):
        peer = lax.rem(row + d, ROWS)
        pltpu.make_async_remote_copy(
            src_ref=ta.at[:, pl.ds(pl.multiple_of(peer * FEAT, FEAT), FEAT)], dst_ref=t_all.at[row],
            send_sem=all_send.at[1], recv_sem=all_recv.at[1],
            device_id={"row": peer}, device_id_type=MESH,
        ).start()

    product(5, a_all, True)
    product(6, a_all, True)

    def terms(acc, g, u_y, u_z, base, width):
        acc = list(acc)
        for c in range(0, width, 128):
            grad = g[:, c:c + 128].astype(F32)
            for k in range(RITZ):
                acc[k] += grad * up[k, u_y, u_z, :, base + c:base + c + 128]
        return tuple(acc)

    def z_slot(slot):
        step = (slot + 1) // 2
        sign = 1 - 2 * lax.rem(slot, 2)
        return lax.rem(z + sign * step + NZ, NZ)

    def y_slot(slot):
        step = (slot + 1) // 2
        sign = 1 - 2 * lax.rem(slot, 2)
        return lax.rem(y + sign * step + NY, NY)

    def over_z(acc, yi, lo, hi):
        return lax.fori_loop(
            lo, hi, lambda s, a: terms(a, g_z.at[yi, s], yi, z_slot(s), 0, GZ), acc
        )

    def over_y(acc, zi, lo, hi):
        return lax.fori_loop(
            lo, hi, lambda s, a: terms(a, g_y.at[s, zi], y_slot(s), zi, GZ, GY), acc
        )

    acc = (jnp.zeros((8, 128), F32),) * RITZ
    acc = over_z(acc, y, 0, 8)
    acc = over_z(acc, at_y(1), 0, 8)
    acc = over_z(acc, at_y(-1), 0, 8)
    arrived(yz0)
    for step in range(-3, 5):
        acc = over_y(acc, at_z(step), 0, 1)
    for step in range(-3, 4):
        acc = over_y(acc, at_z(step), 1, 4)
    for part in (zo0, zo1, zo2, zo3):
        arrived(part)
    acc = over_z(acc, at_y(2), 0, 8)
    arrived(yg0)
    acc = over_y(acc, at_z(4), 1, 4)

    line = lax.broadcasted_iota(jnp.int32, (8, 128), 0)
    mine = jnp.zeros((8, 128), F32)
    for k in range(RITZ):
        mine = jnp.where(line == k, jnp.sum(acc[k], axis=0, keepdims=True), mine)
    c_col[col] = mine
    spread(c_col.at[col], c_col.at[col], 2, "col", COLS)
    t_done = spread_done(t_all, 1, "row", ROWS)
    t_done.wait_recv()
    for c in range(3):
        product(c, t_all, False)
    spread_done(c_col, 2, "col", COLS).wait_recv()
    mine = c_col[0]
    for i in range(1, COLS):
        mine += c_col[i]
    c_row[row] = mine
    spread(c_row.at[row], c_row.at[row], 3, "row", ROWS)
    for c in range(3, 7):
        product(c, t_all, False)
    spread_done(c_row, 3, "row", ROWS).wait_recv()
    total = jnp.sum(c_row[...], axis=0)
    weights = []
    for k in range(RITZ):
        coeff = jnp.sum(jnp.where(line == k, total, 0.0), axis=(0, 1), keepdims=True)
        scale = jnp.full((1, 1), eig[k], F32) * math.sqrt(QUERY * D_OUT)
        weights.append(coeff / scale)

    def local(yi, zi, lo, width):
        part = pl.ds(lo, width)
        out = weights[0] * up[0, yi, zi, :, part]
        for k in range(1, RITZ):
            out += weights[k] * up[k, yi, zi, :, part]
        return out

    half_z, half_y = SZ // 2, SY // 2

    def chain(send, recv, fill, hops, base, dev, place):
        waits = []

        def step(hop):
            if hop > 0:
                waits[hop - 1].wait_recv()
            fill(send.at[base + hop], recv.at[base + hop - 1] if hop > 0 else None, place(hops - hop))
            waits.append(wire.put(send.at[base + hop], recv.at[base + hop], recv.at[base + hop], dev))

        return step, waits

    def fill_z1(lo):
        def fill(out, got, dest):
            @pl.loop(0, NY)
            def _(i):
                value = local(i, dest, lo, half_z)
                out[i] = value if got is None else value + got[i]
        return fill

    def fill_y1(lo):
        def fill(out, got, dest):
            @pl.loop(0, NZ)
            def _(i):
                value = local(dest, i, lo, half_y)
                out[i] = value if got is None else value + got[i]
        return fill

    za, zaw = chain(z1_send, z1_recv, fill_z1(0), 4, 0, z_dev(1), lambda n: at_z(n))
    zb, zbw = chain(z1_send, z1_recv, fill_z1(half_z), 4, 4, z_dev(-1), lambda n: at_z(-n))
    zc, zcw = chain(z1_send, z1_recv, fill_z1(half_z), 3, 8, z_dev(1), lambda n: at_z(n))
    zd, zdw = chain(z1_send, z1_recv, fill_z1(0), 3, 11, z_dev(-1), lambda n: at_z(-n))
    ya, yaw = chain(y1_send, y1_recv, fill_y1(SZ), 2, 0, y_dev(1), lambda n: at_y(n))
    yb, ybw = chain(y1_send, y1_recv, fill_y1(SZ + half_y), 2, 2, y_dev(-1), lambda n: at_y(-n))
    yc, ycw = chain(y1_send, y1_recv, fill_y1(SZ + half_y), 1, 4, y_dev(1), lambda n: at_y(n))
    yd, ydw = chain(y1_send, y1_recv, fill_y1(SZ), 1, 5, y_dev(-1), lambda n: at_y(-n))
    za(0), zb(0), ya(0), yb(0), zc(0), zd(0), yc(0), yd(0)
    za(1), zb(1), zc(1), zd(1)
    za(2), zb(2), ya(1), yb(1), zc(2), zd(2)
    za(3), zb(3)

    zdw[2].wait_recv(), zcw[2].wait_recv(), ydw[0].wait_recv(), ycw[0].wait_recv()

    def fold_y():
        @pl.loop(0, NZ)
        def _(i):
            y2[i, :, 0:half_y] = local(y, i, SZ, half_y) + y1_recv[1, i] + y1_recv[5, i]
            y2[i, :, half_y:SY] = local(y, i, SZ + half_y, half_y) + y1_recv[3, i] + y1_recv[4, i]

    def fold_z():
        @pl.loop(0, NY)
        def _(i):
            z2[i, :, 0:half_z] = local(i, z, 0, half_z) + z1_recv[3, i] + z1_recv[13, i]
            z2[i, :, half_z:SZ] = local(i, z, half_z, half_z) + z1_recv[7, i] + z1_recv[10, i]

    def fill_2(src, part):
        def fill(out, got, dest):
            value = src[dest, :, part]
            out[...] = value if got is None else value + got[...]
        return fill

    low_y, high_y = pl.ds(0, half_y), pl.ds(half_y, half_y)
    low_z, high_z = pl.ds(0, half_z), pl.ds(half_z, half_z)

    zaw[3].wait_recv(), zbw[3].wait_recv()
    fold_z()
    ua, uaw = chain(z2_send, z2_recv, fill_2(z2, low_z), 2, 0, y_dev(1), lambda n: at_y(n))
    ub, ubw = chain(z2_send, z2_recv, fill_2(z2, high_z), 2, 2, y_dev(-1), lambda n: at_y(-n))
    uc, ucw = chain(z2_send, z2_recv, fill_2(z2, high_z), 1, 4, y_dev(1), lambda n: at_y(n))
    ud, udw = chain(z2_send, z2_recv, fill_2(z2, low_z), 1, 5, y_dev(-1), lambda n: at_y(-n))
    ua(0), ub(0), uc(0), ud(0)

    yaw[1].wait_recv(), ybw[1].wait_recv()
    fold_y()
    va, vaw = chain(y2_send, y2_recv, fill_2(y2, low_y), 4, 0, z_dev(1), lambda n: at_z(n))
    vb, vbw = chain(y2_send, y2_recv, fill_2(y2, high_y), 4, 4, z_dev(-1), lambda n: at_z(-n))
    vc, vcw = chain(y2_send, y2_recv, fill_2(y2, high_y), 3, 8, z_dev(1), lambda n: at_z(n))
    vd, vdw = chain(y2_send, y2_recv, fill_2(y2, low_y), 3, 11, z_dev(-1), lambda n: at_z(-n))
    va(0), vb(0), vc(0), vd(0)
    ua(1), ub(1)
    for hop in (1, 2):
        va(hop), vb(hop), vc(hop), vd(hop)
    va(3), vb(3)

    score = jnp.zeros((8, 128), F32)

    def finish(value, lo, width, score):
        response[:, lo:lo + width] = value.astype(BF16)
        value = value * tg_buf[:, lo:lo + width].astype(F32)
        for c in range(0, width, 128):
            score += value[:, c:c + 128]
        return score

    uaw[1].wait_recv(), udw[0].wait_recv()
    score = finish(z2[y, :, 0:half_z] + z2_recv[1] + z2_recv[5], 0, half_z, score)
    ubw[1].wait_recv(), ucw[0].wait_recv()
    score = finish(z2[y, :, half_z:SZ] + z2_recv[3] + z2_recv[4], half_z, half_z, score)
    vaw[3].wait_recv(), vdw[2].wait_recv()
    score = finish(y2[z, :, 0:half_y] + y2_recv[3] + y2_recv[13], SZ, half_y, score)
    vbw[3].wait_recv(), vcw[2].wait_recv()
    score = finish(y2[z, :, half_y:SY] + y2_recv[7] + y2_recv[10], SZ + half_y, half_y, score)

    s_col[col] = score
    spread(s_col.at[col], s_col.at[col], 4, "col", COLS)
    spread_done(s_col, 4, "col", COLS).wait_recv()
    total = jnp.sum(jnp.sum(s_col[...], axis=0), axis=1, keepdims=True) / math.sqrt(D_OUT)
    lane = lax.broadcasted_iota(jnp.int32, (8, 128), 1)
    scores[...] = jnp.sum(jnp.where(line == lane, total, 0.0), axis=0, keepdims=True)

    wire.drain()
    for buf, i, axis, count in (
        (a_all, 0, "col", COLS), (t_all, 1, "row", ROWS), (c_col, 2, "col", COLS),
        (c_row, 3, "row", ROWS), (s_col, 4, "col", COLS),
    ):
        spread_done(buf, i, axis, count).wait_send()


def per_device(query_acts, query_grads, ritz_mats, eigenvalues, train_acts, train_grads):
    anywhere = pl.BlockSpec(memory_space=pl.ANY)
    vmem, dma = pltpu.VMEM, pltpu.SemaphoreType.DMA
    response, scores = pl.pallas_call(
        kernel,
        out_shape=(
            jax.ShapeDtypeStruct((OWN, WIDTH), BF16),
            jax.ShapeDtypeStruct((1, 128), F32),
        ),
        in_specs=[anywhere, anywhere, anywhere, pl.BlockSpec(memory_space=pltpu.SMEM), anywhere, anywhere],
        out_specs=(pl.BlockSpec(memory_space=vmem), pl.BlockSpec(memory_space=vmem)),
        scratch_shapes=[
            vmem((RITZ, FEAT, WIDTH), F32),
            vmem((RITZ, 2, FEAT, WIDTH), BF16),
            vmem((RITZ, NY, NZ, OWN, WIDTH), F32),
            vmem((COLS, TOK // COLS, FEAT), BF16),
            vmem((ROWS, OWN, FEAT), BF16),
            vmem((NY, NZ, OWN, GZ), BF16),
            vmem((NY, NZ, OWN, GY), BF16),
            vmem((OWN, WIDTH), BF16),
            vmem((14, NY, OWN, SZ // 2), F32),
            vmem((14, NY, OWN, SZ // 2), F32),
            vmem((6, NZ, OWN, SY // 2), F32),
            vmem((6, NZ, OWN, SY // 2), F32),
            vmem((NY, OWN, SZ), F32),
            vmem((NZ, OWN, SY), F32),
            vmem((6, OWN, SZ // 2), F32),
            vmem((6, OWN, SZ // 2), F32),
            vmem((14, OWN, SY // 2), F32),
            vmem((14, OWN, SY // 2), F32),
            vmem((COLS, 8, 128), F32),
            vmem((ROWS, 8, 128), F32),
            vmem((COLS, 8, 128), F32),
            dma((5 + WIDTH // CHUNK,)),
            dma((N_WIRE,)),
            dma((N_WIRE,)),
            dma((5,)),
            dma((5,)),
        ],
        compiler_params=pltpu.CompilerParams(
            collective_id=0, has_side_effects=True, vmem_limit_bytes=60 * 1024 * 1024
        ),
    )(query_acts, query_grads, ritz_mats, eigenvalues, train_acts, train_grads)
    return response, scores[0, :OWN]


def solution(mesh):
    in_specs = (
        P("col", "row"),
        P("row", "col"),
        P(None, "row", "col"),
        P(),
        P("row", None),
        P("row", "col"),
    )
    out_specs = (P("row", "col"), P("row"))
    return jax.shard_map(
        per_device, mesh=mesh, in_specs=in_specs, out_specs=out_specs, check_vma=False
    )
```

time: 478 us -> 92.7 us (0.19)
  waiting for transfers between devices: 276 us -> 0 us
  blocking collectives: 115 us -> 0 us
  Pallas kernels: 0 us -> 89.4 us
  matrix products: 49.2 us -> 0 us
  between operations: 14.1 us -> 0.64 us
  other arithmetic: 7.81 us -> 0 us
  local copies, waits for them, and re-layouts: 9.87 us -> 2.56 us
  starting transfers between devices: 5.4 us -> 0 us
    unnamed x3 -> x0, waiting for transfers between devices: 212 us -> none
    psum x2 -> x0, blocking collectives: 98.8 us -> none  [the longest x1 80.7 us: per_device(): coeffs = lax.psum(local_terms, ('row', 'col'))]
    pallas_call x0 -> x1, Pallas kernels: none -> 89.4 us  [per_device(): pl.pallas_call(kernel, out_shape=(jax.ShapeDtypeStruct((OWN, WIDTH), BF16...]
    all_gather x1 -> x0, waiting for transfers between devices: 64 us -> none  [per_device(): lax.all_gather(query_grads, 'row', axis=0, tiled=True)]
    dot_general x3 -> x0, matrix products: 49.2 us -> none  [the longest x1 40.2 us: per_device(): combined = jnp.tensordot(weights, ritz_mats, axes=1, precision=highest)]
    all_gather x1 -> x0, blocking collectives: 16 us -> none  [per_device(): acts_all = lax.all_gather(query_acts, 'col', axis=0, tiled=True)]
    unnamed x7 -> x1, local copies, waits for them, and re-layouts: 9.57 us -> 1.44 us
    reduce_sum x2 -> x0, other arithmetic: 7.81 us -> none  [the longest x1 5.27 us: per_device(): local_terms = jnp.sum(ritz_mats * grad_tile[None], axis=(1, 2))]
  transfers between devices with their start and end apart: 3 -> 0, of which waited for: 2 -> 0; matrix products, arithmetic and copies ran while one was open for 8% -> 0% of each run, Pallas kernels for 0% -> 0%
where the time goes in v1:
time: 92.7 us; the launch traced here: 92.6 us
  Pallas kernels  89.4 us (96%)
  local copies, waits for them, and re-layouts  2.56 us (3%)
    pallas_call x1, Pallas kernels, per_device(): pl.pallas_call(kernel, out_shape=(jax.ShapeDtypeStruct((OWN, WIDTH), BF16...  89.4 us

profile of v1, /device:TPU:1, one launch (start us, length us, event | category | flops | bytes accessed | tf_op | source)
XLA Modules:
  0.0 92.6 jit_solution(11810116348833844173)
XLA Ops:
  0.6 89.4 %shard_map.77 = (bf16[8,3584]{1,0:T(8,128)(2,1)}, f32[1,128]{1,0:T(1,128)}) custom-call(bf16[32,256]{1,0:T(8,128)(2,1)} %qa.1, bf16[8,3584]{1,0:T(8,128)(2,1)} %qg.1, f32[3,256,3584]{2,1,0:T(8,128)} %ritz.1, f32[3]{0:T(128)} %eig.1, bf16[8,8192]{1,0:T(8,128)(2,1)} %ta.1, bf16[8,3584]{1,0:T(8,128)(2,1)} %tg.1), custom_call_target="tpu_custom_call" | custom-call | tf_op jit(solution)/shard_map/pallas_call | solution.py:474
  90.0 1.1 %slice_bitcast_fusion = f32[8]{0:T(128)} fusion(f32[1,128]{1,0:T(1,128)} %get-tuple-element.5), kind=kLoop, calls=%fused_computation | loop fusion | bytes 64 | tf_op jit(solution)/shard_map/squeeze | solution.py:514
  91.1 1.4 %copy.9 = bf16[8,3584]{1,0:T(8,128)(2,1)} copy(bf16[8,3584]{1,0:T(8,128)(2,1)} %get-tuple-element.8) | data formatting | bytes 114688

commit v2 on v1

--- a/solution.py
+++ b/solution.py
@@ -21,7 +21,7 @@
 FEAT = 8192 // ROWS
 WIDTH = D_OUT // COLS
 CHUNK = 512
-TILE = 256
+TILE = 512
 
 GZ = 2048
 GY = WIDTH - GZ
@@ -51,12 +51,36 @@
 
 N_WIRE = 96
 
+TOP = 127.0 * 128.0
+
+
+def scale_of(most):
+    most = jnp.maximum(jnp.max(most, axis=1, keepdims=True), 1e-30) * 1.008
+    scale = jnp.broadcast_to(most, (8, 128)).astype(BF16)
+    return scale, TOP / scale.astype(F32)
+
+
+def encode(value):
+    value = jnp.floor(value + 0.5)
+    upper = jnp.floor(value * (1.0 / 128.0))
+    lower = value - 128.0 * upper
+    upper += jnp.where(upper >= 0.0, 128.0, -128.0)
+    return (upper * jnp.exp2(lower - 71.0)).astype(BF16)
+
+
+def decode(code, unit):
+    code = code.astype(F32)
+    lower = jnp.floor(jnp.log2(jnp.abs(code)) + 64.003)
+    upper = jnp.floor(code * jnp.exp2(71.0 - lower) + 0.5)
+    upper -= jnp.where(upper >= 0.0, 128.0, -128.0)
+    return (upper * 128.0 + lower) * unit
+
 
 def kernel(
     qa, qg, ritz, eig, ta, tg,
     response, scores,
     r_buf, hl, up, a_all, t_all, g_z, g_y, tg_buf,
-    z1_send, z1_recv, y1_send, y1_recv, z2, y2, z2_send, z2_recv, y2_send, y2_recv,
+    z1_send, z1_recv, y1_send, y1_recv, z2, y2, z2_send, z2_recv, y2_send, y2_recv, work,
     c_col, c_row, s_col,
     load_sem, wire_send, wire_recv, all_send, all_recv,
 ):
@@ -95,11 +119,8 @@
 
     barrier = pltpu.get_barrier_semaphore()
 
-    @pl.loop(1, ROWS)
-    def _(d):
-        pl.semaphore_signal(
-            barrier, inc=1, device_id={"row": lax.rem(row + d, ROWS)}, device_id_type=MESH
-        )
+    for device in (z_dev(1), z_dev(-1), y_dev(1), y_dev(-1)):
+        pl.semaphore_signal(barrier, inc=1, device_id=device, device_id_type=MESH)
 
     @pl.loop(1, COLS)
     def _(d):
@@ -107,7 +128,7 @@
             barrier, inc=1, device_id={"col": lax.rem(col + d, COLS)}, device_id_type=MESH
         )
 
-    pl.semaphore_wait(barrier, ROWS - 1 + COLS - 1)
+    pl.semaphore_wait(barrier, 4 + COLS - 1)
 
     wire = Wire(wire_send, wire_recv)
 
@@ -213,6 +234,16 @@
             )
             up[k, :, :, :, part] = out.reshape(NY, NZ, OWN, TILE)
 
+    def give(first_step, last_step):
+        @pl.loop(first_step * NZ, last_step * NZ)
+        def _(i):
+            peer = lax.rem(y + i // NZ + NY, NY) * NZ + lax.rem(z + lax.rem(i, NZ), NZ)
+            pltpu.make_async_remote_copy(
+                src_ref=ta.at[:, pl.ds(pl.multiple_of(peer * FEAT, FEAT), FEAT)], dst_ref=t_all.at[row],
+                send_sem=all_send.at[1], recv_sem=all_recv.at[1],
+                device_id={"row": peer}, device_id_type=MESH,
+            ).start()
+
     zz0 = zz(0)
     yy0 = yy(0)
     spread(qa, a_all.at[col], 0, "col", COLS)
@@ -251,6 +282,16 @@
 
     arrived(zz3)
     zy3 = zy(5, 8)
+
+    @pl.loop(1, NZ)
+    def _(i):
+        peer = y * NZ + lax.rem(z + i, NZ)
+        pltpu.make_async_remote_copy(
+            src_ref=ta.at[:, pl.ds(pl.multiple_of(peer * FEAT, FEAT), FEAT)], dst_ref=t_all.at[row],
+            send_sem=all_send.at[1], recv_sem=all_recv.at[1],
+            device_id={"row": peer}, device_id_type=MESH,
+        ).start()
+
     arrived(zy2)
     zo2 = zy_on(3, 5)
     product(3, a_all, True)
@@ -262,15 +303,8 @@
     arrived(yg0)
     yg0 = yz(1, 4, 3)
 
-    @pl.loop(1, ROWS)
-    def _(d):
-        peer = lax.rem(row + d, ROWS)
-        pltpu.make_async_remote_copy(
-            src_ref=ta.at[:, pl.ds(pl.multiple_of(peer * FEAT, FEAT), FEAT)], dst_ref=t_all.at[row],
-            send_sem=all_send.at[1], recv_sem=all_recv.at[1],
-            device_id={"row": peer}, device_id_type=MESH,
-        ).start()
-
+    give(1, 2)
+    give(3, 4)
     product(5, a_all, True)
     product(6, a_all, True)
 
@@ -313,6 +347,7 @@
         acc = over_y(acc, at_z(step), 1, 4)
     for part in (zo0, zo1, zo2, zo3):
         arrived(part)
+    give(2, 3)
     acc = over_z(acc, at_y(2), 0, 8)
     arrived(yg0)
     acc = over_y(acc, at_z(4), 1, 4)
@@ -323,17 +358,14 @@
         mine = jnp.where(line == k, jnp.sum(acc[k], axis=0, keepdims=True), mine)
     c_col[col] = mine
     spread(c_col.at[col], c_col.at[col], 2, "col", COLS)
-    t_done = spread_done(t_all, 1, "row", ROWS)
-    t_done.wait_recv()
-    for c in range(3):
-        product(c, t_all, False)
     spread_done(c_col, 2, "col", COLS).wait_recv()
     mine = c_col[0]
     for i in range(1, COLS):
         mine += c_col[i]
     c_row[row] = mine
     spread(c_row.at[row], c_row.at[row], 3, "row", ROWS)
-    for c in range(3, 7):
+    spread_done(t_all, 1, "row", ROWS).wait_recv()
+    for c in range(WIDTH // CHUNK):
         product(c, t_all, False)
     spread_done(c_row, 3, "row", ROWS).wait_recv()
     total = jnp.sum(c_row[...], axis=0)
@@ -343,41 +375,57 @@
         scale = jnp.full((1, 1), eig[k], F32) * math.sqrt(QUERY * D_OUT)
         weights.append(coeff / scale)
 
-    def local(yi, zi, lo, width):
-        part = pl.ds(lo, width)
+    half_z, half_y = SZ // 2, SY // 2
+
+    def tile(yi, zi, lo):
+        part = pl.ds(lo, 128)
         out = weights[0] * up[0, yi, zi, :, part]
         for k in range(1, RITZ):
             out += weights[k] * up[k, yi, zi, :, part]
         return out
 
-    half_z, half_y = SZ // 2, SY // 2
-
-    def chain(send, recv, fill, hops, base, dev, place):
+    def fill(blocks, lo, width, source):
+        n = width // 128
+
+        def run(out, got, dest):
+            unit = None if got is None else got[blocks * n].astype(F32) * (1.0 / TOP)
+
+            def add(i, most):
+                for c in range(n):
+                    value = source(i, dest, lo + c * 128)
+                    if got is not None:
+                        value += decode(got[i * n + c], unit)
+                    work[i * n + c] = value
+                    most = jnp.maximum(most, jnp.abs(value))
+                return most
+
+            most = lax.fori_loop(0, blocks, add, jnp.zeros((8, 128), F32))
+            scale, unscale = scale_of(most)
+            out[blocks * n] = scale
+
+            @pl.loop(0, blocks)
+            def _(i):
+                for c in range(n):
+                    out[i * n + c] = encode(work[i * n + c] * unscale)
+
+        return run
+
+    def chain(send, recv, run, hops, base, dev, place):
         waits = []
 
         def step(hop):
             if hop > 0:
                 waits[hop - 1].wait_recv()
-            fill(send.at[base + hop], recv.at[base + hop - 1] if hop > 0 else None, place(hops - hop))
+            run(send.at[base + hop], recv.at[base + hop - 1] if hop > 0 else None, place(hops - hop))
             waits.append(wire.put(send.at[base + hop], recv.at[base + hop], recv.at[base + hop], dev))
 
         return step, waits
 
     def fill_z1(lo):
-        def fill(out, got, dest):
-            @pl.loop(0, NY)
-            def _(i):
-                value = local(i, dest, lo, half_z)
-                out[i] = value if got is None else value + got[i]
-        return fill
+        return fill(NY, lo, half_z, lambda i, dest, at: tile(i, dest, at))
 
     def fill_y1(lo):
-        def fill(out, got, dest):
-            @pl.loop(0, NZ)
-            def _(i):
-                value = local(dest, i, lo, half_y)
-                out[i] = value if got is None else value + got[i]
-        return fill
+        return fill(NZ, lo, half_y, lambda i, dest, at: tile(dest, i, at))
 
     za, zaw = chain(z1_send, z1_recv, fill_z1(0), 4, 0, z_dev(1), lambda n: at_z(n))
     zb, zbw = chain(z1_send, z1_recv, fill_z1(half_z), 4, 4, z_dev(-1), lambda n: at_z(-n))
@@ -387,71 +435,102 @@
     yb, ybw = chain(y1_send, y1_recv, fill_y1(SZ + half_y), 2, 2, y_dev(-1), lambda n: at_y(-n))
     yc, ycw = chain(y1_send, y1_recv, fill_y1(SZ + half_y), 1, 4, y_dev(1), lambda n: at_y(n))
     yd, ydw = chain(y1_send, y1_recv, fill_y1(SZ), 1, 5, y_dev(-1), lambda n: at_y(-n))
+
+    n_z, n_y = SZ // 128, SY // 128
+
+    def fold(i, most, lo, n, place, recv, block, pairs, into):
+        for half, (p, q) in enumerate(pairs):
+            units = [recv[j, block * n].astype(F32) * (1.0 / TOP) for j in (p, q)]
+            for c in range(n):
+                at = half * n + c
+                value = place(i, lo + at * 128)
+                for j, unit in zip((p, q), units):
+                    value += decode(recv[j, i * n + c], unit)
+                into[i, at] = value
+                most = jnp.maximum(most, jnp.abs(value))
+        return most
+
+    def fold_y(i):
+        return fold(
+            i, jnp.zeros((8, 128), F32), SZ, n_y // 2, lambda i, at: tile(y, i, at), y1_recv, NZ,
+            ((1, 5), (3, 4)), y2,
+        )
+
+    def fold_z(i):
+        return fold(
+            i, jnp.zeros((8, 128), F32), 0, n_z // 2, lambda i, at: tile(i, z, at), z1_recv, NY,
+            ((3, 13), (7, 10)), z2,
+        )
+
+    def code_block(src, out, n, most):
+        scale, unscale = scale_of(most)
+        out[n] = scale
+        for c in range(n):
+            out[c] = encode(src[c] * unscale)
+
+    def second_y():
+        @pl.loop(0, NZ - 1)
+        def _(i):
+            far = NZ // 2 + (1 - 2 * lax.rem(i, 2)) * ((i + 1) // 2)
+            dest = lax.rem(z + far, NZ)
+            code_block(y2.at[dest], y2_send.at[dest], n_y, fold_y(dest))
+            pltpu.make_async_remote_copy(
+                src_ref=y2_send.at[dest], dst_ref=y2_recv.at[z], send_sem=all_send.at[5],
+                recv_sem=all_recv.at[5], device_id={"row": y * NZ + dest}, device_id_type=MESH,
+            ).start()
+
+        fold_y(z)
+
+    def second_z():
+        @pl.loop(0, NY - 1)
+        def _(i):
+            far = NY // 2 + (1 - 2 * lax.rem(i, 2)) * ((i + 1) // 2)
+            dest = lax.rem(y + far, NY)
+            code_block(z2.at[dest], z2_send.at[dest], n_z, fold_z(dest))
+            pltpu.make_async_remote_copy(
+                src_ref=z2_send.at[dest], dst_ref=z2_recv.at[y], send_sem=all_send.at[6],
+                recv_sem=all_recv.at[6], device_id={"row": dest * NZ + z}, device_id_type=MESH,
+            ).start()
+
+        fold_z(y)
+
+    def second_done(buf, i):
+        whole = buf.at[pl.ds(0, buf.shape[0] - 1)]
+        return pltpu.make_async_remote_copy(
+            src_ref=whole, dst_ref=whole, send_sem=all_send.at[i], recv_sem=all_recv.at[i],
+            device_id={"row": 0}, device_id_type=MESH,
+        )
+
     za(0), zb(0), ya(0), yb(0), zc(0), zd(0), yc(0), yd(0)
     za(1), zb(1), zc(1), zd(1)
-    za(2), zb(2), ya(1), yb(1), zc(2), zd(2)
+    ya(1), yb(1)
+    za(2), zb(2), zc(2), zd(2)
+    ydw[0].wait_recv(), ycw[0].wait_recv()
+    yaw[1].wait_recv(), ybw[1].wait_recv()
     za(3), zb(3)
-
-    zdw[2].wait_recv(), zcw[2].wait_recv(), ydw[0].wait_recv(), ycw[0].wait_recv()
-
-    def fold_y():
-        @pl.loop(0, NZ)
-        def _(i):
-            y2[i, :, 0:half_y] = local(y, i, SZ, half_y) + y1_recv[1, i] + y1_recv[5, i]
-            y2[i, :, half_y:SY] = local(y, i, SZ + half_y, half_y) + y1_recv[3, i] + y1_recv[4, i]
-
-    def fold_z():
-        @pl.loop(0, NY)
-        def _(i):
-            z2[i, :, 0:half_z] = local(i, z, 0, half_z) + z1_recv[3, i] + z1_recv[13, i]
-            z2[i, :, half_z:SZ] = local(i, z, half_z, half_z) + z1_recv[7, i] + z1_recv[10, i]
-
-    def fill_2(src, part):
-        def fill(out, got, dest):
-            value = src[dest, :, part]
-            out[...] = value if got is None else value + got[...]
-        return fill
-
-    low_y, high_y = pl.ds(0, half_y), pl.ds(half_y, half_y)
-    low_z, high_z = pl.ds(0, half_z), pl.ds(half_z, half_z)
-
+    second_y()
+    zdw[2].wait_recv(), zcw[2].wait_recv()
     zaw[3].wait_recv(), zbw[3].wait_recv()
-    fold_z()
-    ua, uaw = chain(z2_send, z2_recv, fill_2(z2, low_z), 2, 0, y_dev(1), lambda n: at_y(n))
-    ub, ubw = chain(z2_send, z2_recv, fill_2(z2, high_z), 2, 2, y_dev(-1), lambda n: at_y(-n))
-    uc, ucw = chain(z2_send, z2_recv, fill_2(z2, high_z), 1, 4, y_dev(1), lambda n: at_y(n))
-    ud, udw = chain(z2_send, z2_recv, fill_2(z2, low_z), 1, 5, y_dev(-1), lambda n: at_y(-n))
-    ua(0), ub(0), uc(0), ud(0)
-
-    yaw[1].wait_recv(), ybw[1].wait_recv()
-    fold_y()
-    va, vaw = chain(y2_send, y2_recv, fill_2(y2, low_y), 4, 0, z_dev(1), lambda n: at_z(n))
-    vb, vbw = chain(y2_send, y2_recv, fill_2(y2, high_y), 4, 4, z_dev(-1), lambda n: at_z(-n))
-    vc, vcw = chain(y2_send, y2_recv, fill_2(y2, high_y), 3, 8, z_dev(1), lambda n: at_z(n))
-    vd, vdw = chain(y2_send, y2_recv, fill_2(y2, low_y), 3, 11, z_dev(-1), lambda n: at_z(-n))
-    va(0), vb(0), vc(0), vd(0)
-    ua(1), ub(1)
-    for hop in (1, 2):
-        va(hop), vb(hop), vc(hop), vd(hop)
-    va(3), vb(3)
+    second_z()
+
+    def finish(mine, recv, me, count, n, lo, score):
+        def other(d, held):
+            slot = lax.rem(me + d, count)
+            unit = recv[slot, n].astype(F32) * (1.0 / TOP)
+            return tuple(held[c] + decode(recv[slot, c], unit) for c in range(n))
+
+        held = lax.fori_loop(1, count, other, tuple(mine[me, c] for c in range(n)))
+        for c in range(n):
+            part = pl.ds(lo + c * 128, 128)
+            response[:, part] = held[c].astype(BF16)
+            score += held[c] * tg_buf[:, part].astype(F32)
+        return score
 
     score = jnp.zeros((8, 128), F32)
-
-    def finish(value, lo, width, score):
-        response[:, lo:lo + width] = value.astype(BF16)
-        value = value * tg_buf[:, lo:lo + width].astype(F32)
-        for c in range(0, width, 128):
-            score += value[:, c:c + 128]
-        return score
-
-    uaw[1].wait_recv(), udw[0].wait_recv()
-    score = finish(z2[y, :, 0:half_z] + z2_recv[1] + z2_recv[5], 0, half_z, score)
-    ubw[1].wait_recv(), ucw[0].wait_recv()
-    score = finish(z2[y, :, half_z:SZ] + z2_recv[3] + z2_recv[4], half_z, half_z, score)
-    vaw[3].wait_recv(), vdw[2].wait_recv()
-    score = finish(y2[z, :, 0:half_y] + y2_recv[3] + y2_recv[13], SZ, half_y, score)
-    vbw[3].wait_recv(), vcw[2].wait_recv()
-    score = finish(y2[z, :, half_y:SY] + y2_recv[7] + y2_recv[10], SZ + half_y, half_y, score)
+    second_done(y2_recv, 5).wait_recv()
+    score = finish(y2, y2_recv, z, NZ, n_y, SZ, score)
+    second_done(z2_recv, 6).wait_recv()
+    score = finish(z2, z2_recv, y, NY, n_z, 0, score)
 
     s_col[col] = score
     spread(s_col.at[col], s_col.at[col], 4, "col", COLS)
@@ -466,6 +545,8 @@
         (c_row, 3, "row", ROWS), (s_col, 4, "col", COLS),
     ):
         spread_done(buf, i, axis, count).wait_send()
+    second_done(y2_send, 5).wait_send()
+    second_done(z2_send, 6).wait_send()
 
 
 def per_device(query_acts, query_grads, ritz_mats, eigenvalues, train_acts, train_grads):
@@ -488,24 +569,25 @@
             vmem((NY, NZ, OWN, GZ), BF16),
             vmem((NY, NZ, OWN, GY), BF16),
             vmem((OWN, WIDTH), BF16),
-            vmem((14, NY, OWN, SZ // 2), F32),
-            vmem((14, NY, OWN, SZ // 2), F32),
-            vmem((6, NZ, OWN, SY // 2), F32),
-            vmem((6, NZ, OWN, SY // 2), F32),
-            vmem((NY, OWN, SZ), F32),
-            vmem((NZ, OWN, SY), F32),
-            vmem((6, OWN, SZ // 2), F32),
-            vmem((6, OWN, SZ // 2), F32),
-            vmem((14, OWN, SY // 2), F32),
-            vmem((14, OWN, SY // 2), F32),
+            vmem((14, NY * SZ // 256 + 1, OWN, 128), BF16),
+            vmem((14, NY * SZ // 256 + 1, OWN, 128), BF16),
+            vmem((6, NZ * SY // 256 + 1, OWN, 128), BF16),
+            vmem((6, NZ * SY // 256 + 1, OWN, 128), BF16),
+            vmem((NY, SZ // 128, OWN, 128), F32),
+            vmem((NZ, SY // 128, OWN, 128), F32),
+            vmem((NY, SZ // 128 + 1, OWN, 128), BF16),
+            vmem((NY, SZ // 128 + 1, OWN, 128), BF16),
+            vmem((NZ, SY // 128 + 1, OWN, 128), BF16),
+            vmem((NZ, SY // 128 + 1, OWN, 128), BF16),
+            vmem((NZ * SY // 256, OWN, 128), F32),
             vmem((COLS, 8, 128), F32),
             vmem((ROWS, 8, 128), F32),
             vmem((COLS, 8, 128), F32),
             dma((5 + WIDTH // CHUNK,)),
             dma((N_WIRE,)),
             dma((N_WIRE,)),
-            dma((5,)),
-            dma((5,)),
+            dma((7,)),
+            dma((7,)),
         ],
         compiler_params=pltpu.CompilerParams(
             collective_id=0, has_side_effects=True, vmem_limit_bytes=60 * 1024 * 1024

time: 92.7 us -> 78.5 us (0.85)
  Pallas kernels: 89.4 us -> 74.7 us
    pallas_call x1, Pallas kernels: 89.4 us -> 74.7 us  [per_device(): pl.pallas_call(kernel, out_shape=(jax.ShapeDtypeStruct((OWN, WIDTH), BF16...]
where the time goes in v2:
time: 78.5 us; the launch traced here: 77.9 us
  Pallas kernels  74.7 us (95%)
  local copies, waits for them, and re-layouts  2.56 us (3%)
    pallas_call x1, Pallas kernels, per_device(): pl.pallas_call(kernel, out_shape=(jax.ShapeDtypeStruct((OWN, WIDTH), BF16...  74.7 us

profile of v2, /device:TPU:1, one launch (start us, length us, event | category | flops | bytes accessed | tf_op | source)
XLA Modules:
  0.0 77.9 jit_solution(8029555780906904656)
XLA Ops:
  0.6 74.7 %shard_map.77 = (bf16[8,3584]{1,0:T(8,128)(2,1)}, f32[1,128]{1,0:T(1,128)}) custom-call(bf16[32,256]{1,0:T(8,128)(2,1)} %qa.1, bf16[8,3584]{1,0:T(8,128)(2,1)} %qg.1, f32[3,256,3584]{2,1,0:T(8,128)} %ritz.1, f32[3]{0:T(128)} %eig.1, bf16[8,8192]{1,0:T(8,128)(2,1)} %ta.1, bf16[8,3584]{1,0:T(8,128)(2,1)} %tg.1), custom_call_target="tpu_custom_call" | custom-call | tf_op jit(solution)/shard_map/pallas_call | solution.py:555
  75.3 1.1 %slice_bitcast_fusion = f32[8]{0:T(128)} fusion(f32[1,128]{1,0:T(1,128)} %get-tuple-element.5), kind=kLoop, calls=%fused_computation | loop fusion | bytes 64 | tf_op jit(solution)/shard_map/squeeze | solution.py:596
  76.4 1.4 %copy.9 = bf16[8,3584]{1,0:T(8,128)(2,1)} copy(bf16[8,3584]{1,0:T(8,128)(2,1)} %get-tuple-element.8) | data formatting | bytes 114688

commit v3 on v2

--- a/solution.py
+++ b/solution.py
@@ -23,7 +23,7 @@
 CHUNK = 512
 TILE = 512
 
-GZ = 2048
+GZ = 2560
 GY = WIDTH - GZ
 SZ = 1536
 SY = WIDTH - SZ
@@ -119,7 +119,8 @@
 
     barrier = pltpu.get_barrier_semaphore()
 
-    for device in (z_dev(1), z_dev(-1), y_dev(1), y_dev(-1)):
+    near = (z_dev(1), z_dev(-1), z_dev(2), z_dev(-2), y_dev(1), y_dev(-1), y_dev(2))
+    for device in near:
         pl.semaphore_signal(barrier, inc=1, device_id=device, device_id_type=MESH)
 
     @pl.loop(1, COLS)
@@ -128,7 +129,7 @@
             barrier, inc=1, device_id={"col": lax.rem(col + d, COLS)}, device_id_type=MESH
         )
 
-    pl.semaphore_wait(barrier, 4 + COLS - 1)
+    pl.semaphore_wait(barrier, len(near) + COLS - 1)
 
     wire = Wire(wire_send, wire_recv)
 
@@ -152,18 +153,19 @@
     first, second = pl.ds(0, GZ // 2), pl.ds(GZ // 2, GZ // 2)
     y_first, y_second = pl.ds(0, GY // 2), pl.ds(GY // 2, GY // 2)
 
-    def zz(hop):
-        if hop < 3:
-            src_r, dst_r = max(2 * hop - 1, 0), 2 * hop + 1
-            src_l, dst_l = 2 * hop, 2 * hop + 2
-            own = qg.at[:, pl.ds(0, GZ)]
-            return (
-                wire.put(own if hop == 0 else g_z.at[y, src_r], g_z.at[y, dst_r], g_z.at[y, dst_r], z_dev(1)),
-                wire.put(own if hop == 0 else g_z.at[y, src_l], g_z.at[y, dst_l], g_z.at[y, dst_l], z_dev(-1)),
-            )
+    def zz_near(step):
+        own = qg.at[:, pl.ds(0, GZ)]
+        right, left = g_z.at[y, 2 * step - 1], g_z.at[y, 2 * step]
+        return (wire.put(own, right, right, z_dev(step)), wire.put(own, left, left, z_dev(-step)))
+
+    def zz_far():
+        right, left = g_z.at[y, 3], g_z.at[y, 4]
+        last = g_z.at[y, 7, :, first], g_z.at[y, 7, :, second]
         return (
-            wire.put(g_z.at[y, 5, :, first], g_z.at[y, 7, :, first], g_z.at[y, 7, :, first], z_dev(1)),
-            wire.put(g_z.at[y, 6, :, second], g_z.at[y, 7, :, second], g_z.at[y, 7, :, second], z_dev(-1)),
+            wire.put(right, g_z.at[y, 5], g_z.at[y, 5], z_dev(1)),
+            wire.put(left, g_z.at[y, 6], g_z.at[y, 6], z_dev(-1)),
+            wire.put(g_z.at[y, 3, :, first], last[0], last[0], z_dev(2)),
+            wire.put(g_z.at[y, 4, :, second], last[1], last[1], z_dev(-2)),
         )
 
     def zy(lo, hi):
@@ -188,25 +190,31 @@
             ),
         )
 
-    def yy(hop):
-        if hop == 0:
-            own = qg.at[:, pl.ds(GZ, GY)]
-            return (
-                wire.put(own, g_y.at[1, z], g_y.at[1, z], y_dev(1)),
-                wire.put(own, g_y.at[2, z], g_y.at[2, z], y_dev(-1)),
-            )
+    def yy():
+        own = qg.at[:, pl.ds(GZ, GY)]
+        return tuple(
+            wire.put(own, g_y.at[slot, z], g_y.at[slot, z], y_dev(step))
+            for slot, step in ((3, 2), (1, 1), (2, -1))
+        )
+
+    def yz_near(lo, hi, step):
+        slots = pl.ds(lo, hi - lo)
+        src = g_y.at[slots, z]
         return (
-            wire.put(g_y.at[1, z, :, y_first], g_y.at[3, z, :, y_first], g_y.at[3, z, :, y_first], y_dev(1)),
-            wire.put(g_y.at[2, z, :, y_second], g_y.at[3, z, :, y_second], g_y.at[3, z, :, y_second], y_dev(-1)),
-        )
-
-    def yz(lo, hi, hop):
+            wire.put(src, src, g_y.at[slots, at_z(-step)], z_dev(step)),
+            wire.put(src, src, g_y.at[slots, at_z(step)], z_dev(-step)),
+        )
+
+    def yz_far(lo, hi):
         slots = pl.ds(lo, hi - lo)
-        right = g_y.at[slots, at_z(-hop)] if hop < 3 else g_y.at[slots, at_z(-hop), :, y_first]
-        left = g_y.at[slots, at_z(hop)] if hop < 3 else g_y.at[slots, at_z(hop), :, y_second]
-        land_r = g_y.at[slots, at_z(-hop - 1)] if hop < 3 else g_y.at[slots, at_z(-hop - 1), :, y_first]
-        land_l = g_y.at[slots, at_z(hop + 1)] if hop < 3 else g_y.at[slots, at_z(hop + 1), :, y_second]
-        return (wire.put(right, right, land_r, z_dev(1)), wire.put(left, left, land_l, z_dev(-1)))
+        right, left = g_y.at[slots, at_z(-2)], g_y.at[slots, at_z(2)]
+        half_r, half_l = g_y.at[slots, at_z(-2), :, y_first], g_y.at[slots, at_z(2), :, y_second]
+        return (
+            wire.put(right, right, g_y.at[slots, at_z(-3)], z_dev(1)),
+            wire.put(left, left, g_y.at[slots, at_z(3)], z_dev(-1)),
+            wire.put(half_r, half_r, g_y.at[slots, at_z(-4), :, y_first], z_dev(2)),
+            wire.put(half_l, half_l, g_y.at[slots, at_z(4), :, y_second], z_dev(-2)),
+        )
 
     def arrived(copies):
         for copy in copies:
@@ -235,7 +243,7 @@
             up[k, :, :, :, part] = out.reshape(NY, NZ, OWN, TILE)
 
     def give(first_step, last_step):
-        @pl.loop(first_step * NZ, last_step * NZ)
+        @pl.loop(max(first_step * NZ, 1), last_step * NZ)
         def _(i):
             peer = lax.rem(y + i // NZ + NY, NY) * NZ + lax.rem(z + lax.rem(i, NZ), NZ)
             pltpu.make_async_remote_copy(
@@ -244,65 +252,41 @@
                 device_id={"row": peer}, device_id_type=MESH,
             ).start()
 
-    zz0 = zz(0)
-    yy0 = yy(0)
-    spread(qa, a_all.at[col], 0, "col", COLS)
+    zz_2 = zz_near(2)
+    yy_all = yy()
+    zz_1 = zz_near(1)
     for load in loads[:n_small]:
         load.wait()
-    zy0 = zy(0, 1)
-    yz0 = yz(0, 1, 0)
-    arrived(zz0)
-    zz1, zy1 = zz(1), zy(1, 3)
-    arrived(yy0)
-    yy1 = yy(1)
-    arrived(yz0)
-    yz0 = yz(0, 1, 1)
+    zy_0 = zy(0, 1)
+    own_2, own_1 = yz_near(0, 1, 2), yz_near(0, 1, 1)
+    spread(qa, a_all.at[col], 0, "col", COLS)
+    arrived(zz_2)
+    zz_3 = zz_far()
+    arrived(yy_all)
+    rest_2, rest_1 = yz_near(1, 4, 2), yz_near(1, 4, 1)
+    arrived(zz_1)
+    zy_1, zy_2 = zy(1, 3), zy(3, 5)
     spread_done(a_all, 0, "col", COLS).wait_recv()
     product(0, a_all, True)
-
-    arrived(zz1)
-    zz2, zy2 = zz(2), zy(3, 5)
-    arrived(zy0)
-    zo0 = zy_on(0, 1)
-    arrived(yy1)
-    yg0 = yz(1, 4, 0)
-    arrived(yz0)
-    yz0 = yz(0, 1, 2)
+    arrived(zy_0)
+    on_0 = zy_on(0, 1)
+    arrived(own_2)
+    own_3 = yz_far(0, 1)
     product(1, a_all, True)
-
-    arrived(zz2)
-    zz3 = zz(3)
-    arrived(zy1)
-    zo1 = zy_on(1, 3)
-    arrived(yz0)
-    yz0 = yz(0, 1, 3)
-    arrived(yg0)
-    yg0 = yz(1, 4, 1)
+    arrived(zz_3)
+    zy_3 = zy(5, 8)
     product(2, a_all, True)
-
-    arrived(zz3)
-    zy3 = zy(5, 8)
-
-    @pl.loop(1, NZ)
-    def _(i):
-        peer = y * NZ + lax.rem(z + i, NZ)
-        pltpu.make_async_remote_copy(
-            src_ref=ta.at[:, pl.ds(pl.multiple_of(peer * FEAT, FEAT), FEAT)], dst_ref=t_all.at[row],
-            send_sem=all_send.at[1], recv_sem=all_recv.at[1],
-            device_id={"row": peer}, device_id_type=MESH,
-        ).start()
-
-    arrived(zy2)
-    zo2 = zy_on(3, 5)
+    arrived(rest_2)
+    rest_3 = yz_far(1, 4)
+    arrived(zy_1)
+    on_1 = zy_on(1, 3)
+    give(0, 1)
     product(3, a_all, True)
-    arrived(yg0)
-    yg0 = yz(1, 4, 2)
+    arrived(zy_2)
+    on_2 = zy_on(3, 5)
     product(4, a_all, True)
-    arrived(zy3)
-    zo3 = zy_on(5, 8)
-    arrived(yg0)
-    yg0 = yz(1, 4, 3)
-
+    arrived(zy_3)
+    on_3 = zy_on(5, 8)
     give(1, 2)
     give(3, 4)
     product(5, a_all, True)
@@ -340,17 +324,18 @@
     acc = over_z(acc, y, 0, 8)
     acc = over_z(acc, at_y(1), 0, 8)
     acc = over_z(acc, at_y(-1), 0, 8)
-    arrived(yz0)
+    for part in (own_1, own_3, rest_1):
+        arrived(part)
     for step in range(-3, 5):
         acc = over_y(acc, at_z(step), 0, 1)
-    for step in range(-3, 4):
+    for step in range(-2, 3):
         acc = over_y(acc, at_z(step), 1, 4)
-    for part in (zo0, zo1, zo2, zo3):
+    for part in (on_0, on_1, on_2, rest_3, on_3):
         arrived(part)
     give(2, 3)
+    for step in (-3, 3, 4):
+        acc = over_y(acc, at_z(step), 1, 4)
     acc = over_z(acc, at_y(2), 0, 8)
-    arrived(yg0)
-    acc = over_y(acc, at_z(4), 1, 4)
 
     line = lax.broadcasted_iota(jnp.int32, (8, 128), 0)
     mine = jnp.zeros((8, 128), F32)
@@ -387,13 +372,13 @@
     def fill(blocks, lo, width, source):
         n = width // 128
 
-        def run(out, got, dest):
-            unit = None if got is None else got[blocks * n].astype(F32) * (1.0 / TOP)
+        def run(out, arrivals, dest):
+            arrivals = [(got, got[blocks * n].astype(F32) * (1.0 / TOP)) for got in arrivals]
 
             def add(i, most):
                 for c in range(n):
                     value = source(i, dest, lo + c * 128)
-                    if got is not None:
+                    for got, unit in arrivals:
                         value += decode(got[i * n + c], unit)
                     work[i * n + c] = value
                     most = jnp.maximum(most, jnp.abs(value))
@@ -410,16 +395,27 @@
 
         return run
 
-    def chain(send, recv, run, hops, base, dev, place):
+    def chain(send, recv, run, hops, base, dev, place, skip=None):
         waits = []
+        ahead = []
+
+        def start():
+            slot, far = skip
+            run(send.at[slot], [], place(hops + 1))
+            ahead.append(wire.put(send.at[slot], recv.at[slot], recv.at[slot], far))
 
         def step(hop):
+            arrivals = []
             if hop > 0:
                 waits[hop - 1].wait_recv()
-            run(send.at[base + hop], recv.at[base + hop - 1] if hop > 0 else None, place(hops - hop))
+                arrivals.append(recv.at[base + hop - 1])
+            if hop == 1 and ahead:
+                ahead[0].wait_recv()
+                arrivals.append(recv.at[skip[0]])
+            run(send.at[base + hop], arrivals, place(hops - hop))
             waits.append(wire.put(send.at[base + hop], recv.at[base + hop], recv.at[base + hop], dev))
 
-        return step, waits
+        return step, waits, start
 
     def fill_z1(lo):
         return fill(NY, lo, half_z, lambda i, dest, at: tile(i, dest, at))
@@ -427,14 +423,16 @@
     def fill_y1(lo):
         return fill(NZ, lo, half_y, lambda i, dest, at: tile(dest, i, at))
 
-    za, zaw = chain(z1_send, z1_recv, fill_z1(0), 4, 0, z_dev(1), lambda n: at_z(n))
-    zb, zbw = chain(z1_send, z1_recv, fill_z1(half_z), 4, 4, z_dev(-1), lambda n: at_z(-n))
-    zc, zcw = chain(z1_send, z1_recv, fill_z1(half_z), 3, 8, z_dev(1), lambda n: at_z(n))
-    zd, zdw = chain(z1_send, z1_recv, fill_z1(0), 3, 11, z_dev(-1), lambda n: at_z(-n))
-    ya, yaw = chain(y1_send, y1_recv, fill_y1(SZ), 2, 0, y_dev(1), lambda n: at_y(n))
-    yb, ybw = chain(y1_send, y1_recv, fill_y1(SZ + half_y), 2, 2, y_dev(-1), lambda n: at_y(-n))
-    yc, ycw = chain(y1_send, y1_recv, fill_y1(SZ + half_y), 1, 4, y_dev(1), lambda n: at_y(n))
-    yd, ydw = chain(y1_send, y1_recv, fill_y1(SZ), 1, 5, y_dev(-1), lambda n: at_y(-n))
+    za, zaw, za_start = chain(z1_send, z1_recv, fill_z1(0), 3, 0, z_dev(1), lambda n: at_z(n), (12, z_dev(2)))
+    zb, zbw, zb_start = chain(
+        z1_send, z1_recv, fill_z1(half_z), 3, 3, z_dev(-1), lambda n: at_z(-n), (13, z_dev(-2))
+    )
+    zc, zcw, _ = chain(z1_send, z1_recv, fill_z1(half_z), 3, 6, z_dev(1), lambda n: at_z(n))
+    zd, zdw, _ = chain(z1_send, z1_recv, fill_z1(0), 3, 9, z_dev(-1), lambda n: at_z(-n))
+    ya, yaw, _ = chain(y1_send, y1_recv, fill_y1(SZ), 2, 0, y_dev(1), lambda n: at_y(n))
+    yb, ybw, _ = chain(y1_send, y1_recv, fill_y1(SZ + half_y), 2, 2, y_dev(-1), lambda n: at_y(-n))
+    yc, ycw, _ = chain(y1_send, y1_recv, fill_y1(SZ + half_y), 1, 4, y_dev(1), lambda n: at_y(n))
+    yd, ydw, _ = chain(y1_send, y1_recv, fill_y1(SZ), 1, 5, y_dev(-1), lambda n: at_y(-n))
 
     n_z, n_y = SZ // 128, SY // 128
 
@@ -459,7 +457,7 @@
     def fold_z(i):
         return fold(
             i, jnp.zeros((8, 128), F32), 0, n_z // 2, lambda i, at: tile(i, z, at), z1_recv, NY,
-            ((3, 13), (7, 10)), z2,
+            ((2, 11), (5, 8)), z2,
         )
 
     def code_block(src, out, n, most):
@@ -501,16 +499,17 @@
             device_id={"row": 0}, device_id_type=MESH,
         )
 
-    za(0), zb(0), ya(0), yb(0), zc(0), zd(0), yc(0), yd(0)
+    za_start(), zb_start(), ya(0), yb(0)
+    za(0), zb(0), zc(0), zd(0)
+    yc(0), yd(0)
     za(1), zb(1), zc(1), zd(1)
     ya(1), yb(1)
     za(2), zb(2), zc(2), zd(2)
+    yaw[1].wait_recv(), ybw[1].wait_recv()
     ydw[0].wait_recv(), ycw[0].wait_recv()
-    yaw[1].wait_recv(), ybw[1].wait_recv()
-    za(3), zb(3)
     second_y()
+    zaw[2].wait_recv(), zbw[2].wait_recv()
     zdw[2].wait_recv(), zcw[2].wait_recv()
-    zaw[3].wait_recv(), zbw[3].wait_recv()
     second_z()
 
     def finish(mine, recv, me, count, n, lo, score):

time: 78.5 us -> 73.4 us (0.935)
  Pallas kernels: 74.7 us -> 70.1 us
    pallas_call x1, Pallas kernels: 74.7 us -> 70.1 us  [per_device(): pl.pallas_call(kernel, out_shape=(jax.ShapeDtypeStruct((OWN, WIDTH), BF16...]
where the time goes in v3:
time: 73.4 us; the launch traced here: 73.3 us
  Pallas kernels  70.1 us (96%)
  local copies, waits for them, and re-layouts  2.56 us (3%)
    pallas_call x1, Pallas kernels, per_device(): pl.pallas_call(kernel, out_shape=(jax.ShapeDtypeStruct((OWN, WIDTH), BF16...  70.1 us

profile of v3, /device:TPU:1, one launch (start us, length us, event | category | flops | bytes accessed | tf_op | source)
XLA Modules:
  0.0 73.3 jit_solution(17811988830370044595)
XLA Ops:
  0.6 70.1 %shard_map.77 = (bf16[8,3584]{1,0:T(8,128)(2,1)}, f32[1,128]{1,0:T(1,128)}) custom-call(bf16[32,256]{1,0:T(8,128)(2,1)} %qa.1, bf16[8,3584]{1,0:T(8,128)(2,1)} %qg.1, f32[3,256,3584]{2,1,0:T(8,128)} %ritz.1, f32[3]{0:T(128)} %eig.1, bf16[8,8192]{1,0:T(8,128)(2,1)} %ta.1, bf16[8,3584]{1,0:T(8,128)(2,1)} %tg.1), custom_call_target="tpu_custom_call" | custom-call | tf_op jit(solution)/shard_map/pallas_call | solution.py:554
  70.7 1.1 %slice_bitcast_fusion = f32[8]{0:T(128)} fusion(f32[1,128]{1,0:T(1,128)} %get-tuple-element.5), kind=kLoop, calls=%fused_computation | loop fusion | bytes 64 | tf_op jit(solution)/shard_map/squeeze | solution.py:595
  71.8 1.4 %copy.9 = bf16[8,3584]{1,0:T(8,128)(2,1)} copy(bf16[8,3584]{1,0:T(8,128)(2,1)} %get-tuple-element.8) | data formatting | bytes 114688

commit v4 on v3

--- a/solution.py
+++ b/solution.py
@@ -23,7 +23,7 @@
 CHUNK = 512
 TILE = 512
 
-GZ = 2560
+GZ = 2048
 GY = WIDTH - GZ
 SZ = 1536
 SY = WIDTH - SZ
@@ -82,7 +82,7 @@
     r_buf, hl, up, a_all, t_all, g_z, g_y, tg_buf,
     z1_send, z1_recv, y1_send, y1_recv, z2, y2, z2_send, z2_recv, y2_send, y2_recv, work,
     c_col, c_row, s_col,
-    load_sem, wire_send, wire_recv, all_send, all_recv,
+    load_sem, wire_send, wire_recv, all_send, all_recv, y2_sem, z2_sem,
 ):
     row, col = lax.axis_index("row"), lax.axis_index("col")
     y, z = row // NZ, lax.rem(row, NZ)
@@ -133,14 +133,21 @@
 
     wire = Wire(wire_send, wire_recv)
 
+    def outward(i, count):
+        return count // 2 + (1 - 2 * lax.rem(i, 2)) * ((i + 1) // 2)
+
     def spread(src, dst, i, axis, count):
         me = lax.axis_index(axis)
 
-        @pl.loop(1, count)
+        @pl.loop(0, count - 1)
         def _(d):
+            if axis == "row":
+                peer = lax.rem(y + outward(d // NZ, NY), NY) * NZ + lax.rem(z + outward(lax.rem(d, NZ), NZ), NZ)
+            else:
+                peer = lax.rem(me + 1 + d, count)
             pltpu.make_async_remote_copy(
                 src_ref=src, dst_ref=dst, send_sem=all_send.at[i], recv_sem=all_recv.at[i],
-                device_id={axis: lax.rem(me + d, count)}, device_id_type=MESH,
+                device_id={axis: peer}, device_id_type=MESH,
             ).start()
 
     def spread_done(buf, i, axis, count):
@@ -243,9 +250,9 @@
             up[k, :, :, :, part] = out.reshape(NY, NZ, OWN, TILE)
 
     def give(first_step, last_step):
-        @pl.loop(max(first_step * NZ, 1), last_step * NZ)
+        @pl.loop(first_step * NZ, last_step * NZ - (first_step == 0))
         def _(i):
-            peer = lax.rem(y + i // NZ + NY, NY) * NZ + lax.rem(z + lax.rem(i, NZ), NZ)
+            peer = lax.rem(y + i // NZ + NY, NY) * NZ + lax.rem(z + outward(lax.rem(i, NZ), NZ), NZ)
             pltpu.make_async_remote_copy(
                 src_ref=ta.at[:, pl.ds(pl.multiple_of(peer * FEAT, FEAT), FEAT)], dst_ref=t_all.at[row],
                 send_sem=all_send.at[1], recv_sem=all_recv.at[1],
@@ -330,12 +337,15 @@
         acc = over_y(acc, at_z(step), 0, 1)
     for step in range(-2, 3):
         acc = over_y(acc, at_z(step), 1, 4)
-    for part in (on_0, on_1, on_2, rest_3, on_3):
+    for part in (on_0, on_1, on_2):
         arrived(part)
-    give(2, 3)
+    acc = over_z(acc, at_y(2), 0, 5)
+    arrived(rest_3)
     for step in (-3, 3, 4):
         acc = over_y(acc, at_z(step), 1, 4)
-    acc = over_z(acc, at_y(2), 0, 8)
+    arrived(on_3)
+    give(2, 3)
+    acc = over_z(acc, at_y(2), 5, 8)
 
     line = lax.broadcasted_iota(jnp.int32, (8, 128), 0)
     mine = jnp.zeros((8, 128), F32)
@@ -469,12 +479,12 @@
     def second_y():
         @pl.loop(0, NZ - 1)
         def _(i):
-            far = NZ // 2 + (1 - 2 * lax.rem(i, 2)) * ((i + 1) // 2)
+            far = outward(i, NZ)
             dest = lax.rem(z + far, NZ)
             code_block(y2.at[dest], y2_send.at[dest], n_y, fold_y(dest))
             pltpu.make_async_remote_copy(
                 src_ref=y2_send.at[dest], dst_ref=y2_recv.at[z], send_sem=all_send.at[5],
-                recv_sem=all_recv.at[5], device_id={"row": y * NZ + dest}, device_id_type=MESH,
+                recv_sem=y2_sem.at[far], device_id={"row": y * NZ + dest}, device_id_type=MESH,
             ).start()
 
         fold_y(z)
@@ -482,12 +492,12 @@
     def second_z():
         @pl.loop(0, NY - 1)
         def _(i):
-            far = NY // 2 + (1 - 2 * lax.rem(i, 2)) * ((i + 1) // 2)
+            far = outward(i, NY)
             dest = lax.rem(y + far, NY)
             code_block(z2.at[dest], z2_send.at[dest], n_z, fold_z(dest))
             pltpu.make_async_remote_copy(
                 src_ref=z2_send.at[dest], dst_ref=z2_recv.at[y], send_sem=all_send.at[6],
-                recv_sem=all_recv.at[6], device_id={"row": dest * NZ + z}, device_id_type=MESH,
+                recv_sem=z2_sem.at[far], device_id={"row": dest * NZ + z}, device_id_type=MESH,
             ).start()
 
         fold_z(y)
@@ -499,8 +509,8 @@
             device_id={"row": 0}, device_id_type=MESH,
         )
 
-    za_start(), zb_start(), ya(0), yb(0)
-    za(0), zb(0), zc(0), zd(0)
+    za_start(), zb_start(), za(0), zb(0)
+    ya(0), yb(0), zc(0), zd(0)
     yc(0), yd(0)
     za(1), zb(1), zc(1), zd(1)
     ya(1), yb(1)
@@ -512,13 +522,19 @@
     zdw[2].wait_recv(), zcw[2].wait_recv()
     second_z()
 
-    def finish(mine, recv, me, count, n, lo, score):
-        def other(d, held):
-            slot = lax.rem(me + d, count)
-            unit = recv[slot, n].astype(F32) * (1.0 / TOP)
-            return tuple(held[c] + decode(recv[slot, c], unit) for c in range(n))
-
-        held = lax.fori_loop(1, count, other, tuple(mine[me, c] for c in range(n)))
+    def finish(mine, recv, sems, me, count, n, lo, score):
+        def other(i, held):
+            far = outward(i, count)
+            slot = lax.rem(me - far + count, count)
+            block = recv.at[slot]
+            pltpu.make_async_remote_copy(
+                src_ref=block, dst_ref=block, send_sem=all_send.at[5], recv_sem=sems.at[far],
+                device_id={"row": 0}, device_id_type=MESH,
+            ).wait_recv()
+            unit = block[n].astype(F32) * (1.0 / TOP)
+            return tuple(held[c] + decode(block[c], unit) for c in range(n))
+
+        held = lax.fori_loop(0, count - 1, other, tuple(mine[me, c] for c in range(n)))
         for c in range(n):
             part = pl.ds(lo + c * 128, 128)
             response[:, part] = held[c].astype(BF16)
@@ -526,10 +542,8 @@
         return score
 
     score = jnp.zeros((8, 128), F32)
-    second_done(y2_recv, 5).wait_recv()
-    score = finish(y2, y2_recv, z, NZ, n_y, SZ, score)
-    second_done(z2_recv, 6).wait_recv()
-    score = finish(z2, z2_recv, y, NY, n_z, 0, score)
+    score = finish(y2, y2_recv, y2_sem, z, NZ, n_y, SZ, score)
+    score = finish(z2, z2_recv, z2_sem, y, NY, n_z, 0, score)
 
     s_col[col] = score
     spread(s_col.at[col], s_col.at[col], 4, "col", COLS)
@@ -546,6 +560,11 @@
         spread_done(buf, i, axis, count).wait_send()
     second_done(y2_send, 5).wait_send()
     second_done(z2_send, 6).wait_send()
+
+
+def hand_on(response, scores, response_out, scores_out):
+    response_out[...] = response[...]
+    scores_out[...] = scores[:, :OWN]
 
 
 def per_device(query_acts, query_grads, ritz_mats, eigenvalues, train_acts, train_grads):
@@ -587,12 +606,23 @@
             dma((N_WIRE,)),
             dma((7,)),
             dma((7,)),
+            dma((NZ,)),
+            dma((NY,)),
         ],
         compiler_params=pltpu.CompilerParams(
             collective_id=0, has_side_effects=True, vmem_limit_bytes=60 * 1024 * 1024
         ),
     )(query_acts, query_grads, ritz_mats, eigenvalues, train_acts, train_grads)
-    return response, scores[0, :OWN]
+    response, scores = pl.pallas_call(
+        hand_on,
+        out_shape=(
+            jax.ShapeDtypeStruct((OWN, WIDTH), BF16),
+            jax.ShapeDtypeStruct((1, OWN), F32),
+        ),
+        in_specs=[pl.BlockSpec(memory_space=vmem)] * 2,
+        out_specs=(pl.BlockSpec(memory_space=vmem),) * 2,
+    )(response, scores)
+    return response, scores.reshape(OWN)
 
 
 def solution(mesh):

time: 73.4 us -> 71.6 us (0.975)
  local copies, waits for them, and re-layouts: 2.56 us -> 0 us
    pallas_call x0 -> x1, Pallas kernels: none -> 1.45 us  [per_device(): pl.pallas_call(hand_on, out_shape=(jax.ShapeDtypeStruct((OWN, WIDTH), BF1...]
    unnamed x1 -> x0, local copies, waits for them, and re-layouts: 1.44 us -> none
    squeeze x1 -> x0, local copies, waits for them, and re-layouts: 1.12 us -> none  [per_device(): return (response, scores[0, :OWN])]
    pallas_call x1, Pallas kernels: 70.1 us -> 69.3 us  [per_device(): pl.pallas_call(kernel, out_shape=(jax.ShapeDtypeStruct((OWN, WIDTH), BF16...]
where the time goes in v4:
time: 71.6 us; the launch traced here: 71.4 us
  Pallas kernels  70.8 us (99%)
    pallas_call x1, Pallas kernels, per_device(): pl.pallas_call(kernel, out_shape=(jax.ShapeDtypeStruct((OWN, WIDTH), BF16...  69.3 us
    pallas_call x1, Pallas kernels, per_device(): pl.pallas_call(hand_on, out_shape=(jax.ShapeDtypeStruct((OWN, WIDTH), BF1...  1.45 us

profile of v4, /device:TPU:1, one launch (start us, length us, event | category | flops | bytes accessed | tf_op | source)
XLA Modules:
  0.0 71.4 jit_solution(13913209991237487623)
XLA Ops:
  0.6 69.3 %shard_map.77 = (bf16[8,3584]{1,0:T(8,128)(2,1)}, f32[1,128]{1,0:T(1,128)}) custom-call(bf16[32,256]{1,0:T(8,128)(2,1)} %qa.1, bf16[8,3584]{1,0:T(8,128)(2,1)} %qg.1, f32[3,256,3584]{2,1,0:T(8,128)} %ritz.1, f32[3]{0:T(128)} %eig.1, bf16[8,8192]{1,0:T(8,128)(2,1)} %ta.1, bf16[8,3584]{1,0:T(8,128)(2,1)} %tg.1), custom_call_target="tpu_custom_call" | custom-call | tf_op jit(solution)/shard_map/pallas_call | solution.py:573
  70.0 1.5 %shard_map.78 = (bf16[8,3584]{1,0:T(8,128)(2,1)}, f32[1,8]{1,0:T(1,128)}) custom-call(bf16[8,3584]{1,0:T(8,128)(2,1)} %get-tuple-element.6.response, f32[1,128]{1,0:T(1,128)} %get-tuple-element.7.scores), custom_call_target="tpu_custom_call" | custom-call | tf_op jit(solution)/shard_map/pallas_call | solution.py:616

commit v5 on v4

--- a/solution.py
+++ b/solution.py
@@ -141,10 +141,7 @@
 
         @pl.loop(0, count - 1)
         def _(d):
-            if axis == "row":
-                peer = lax.rem(y + outward(d // NZ, NY), NY) * NZ + lax.rem(z + outward(lax.rem(d, NZ), NZ), NZ)
-            else:
-                peer = lax.rem(me + 1 + d, count)
+            peer = lax.rem(me + 1 + d, count)
             pltpu.make_async_remote_copy(
                 src_ref=src, dst_ref=dst, send_sem=all_send.at[i], recv_sem=all_recv.at[i],
                 device_id={axis: peer}, device_id_type=MESH,
@@ -231,7 +228,7 @@
         if split:
             loads[n_small + c].wait()
 
-        @pl.loop(0, RITZ * (CHUNK // TILE))
+        @pl.loop(0, RITZ * (CHUNK // TILE), unroll=RITZ)
         def _(i):
             k = i // (CHUNK // TILE)
             part = pl.ds(pl.multiple_of(c * CHUNK + lax.rem(i, CHUNK // TILE) * TILE, TILE), TILE)
@@ -280,8 +277,10 @@
     arrived(own_2)
     own_3 = yz_far(0, 1)
     product(1, a_all, True)
-    arrived(zz_3)
-    zy_3 = zy(5, 8)
+    arrived(zz_3[:2])
+    zy_3 = zy(5, 7)
+    arrived(zz_3[2:])
+    zy_4 = zy(7, 8)
     product(2, a_all, True)
     arrived(rest_2)
     rest_3 = yz_far(1, 4)
@@ -293,7 +292,9 @@
     on_2 = zy_on(3, 5)
     product(4, a_all, True)
     arrived(zy_3)
-    on_3 = zy_on(5, 8)
+    on_3 = zy_on(5, 7)
+    arrived(zy_4)
+    on_3 += zy_on(7, 8)
     give(1, 2)
     give(3, 4)
     product(5, a_all, True)
@@ -368,7 +369,7 @@
     for k in range(RITZ):
         coeff = jnp.sum(jnp.where(line == k, total, 0.0), axis=(0, 1), keepdims=True)
         scale = jnp.full((1, 1), eig[k], F32) * math.sqrt(QUERY * D_OUT)
-        weights.append(coeff / scale)
+        weights.append(jnp.broadcast_to(coeff / scale, (8, 128)))
 
     half_z, half_y = SZ // 2, SY // 2
 
@@ -394,11 +395,11 @@
                     most = jnp.maximum(most, jnp.abs(value))
                 return most
 
-            most = lax.fori_loop(0, blocks, add, jnp.zeros((8, 128), F32))
+            most = lax.fori_loop(0, blocks, add, jnp.zeros((8, 128), F32), unroll=4)
             scale, unscale = scale_of(most)
             out[blocks * n] = scale
 
-            @pl.loop(0, blocks)
+            @pl.loop(0, blocks, unroll=4)
             def _(i):
                 for c in range(n):
                     out[i * n + c] = encode(work[i * n + c] * unscale)

time: 71.6 us -> 69.7 us (0.973)
  Pallas kernels: 70.8 us -> 69 us
    pallas_call x1, Pallas kernels: 69.3 us -> 67.5 us  [per_device(): pl.pallas_call(kernel, out_shape=(jax.ShapeDtypeStruct((OWN, WIDTH), BF16...]
where the time goes in v5:
time: 69.7 us; the launch traced here: 69.6 us
  Pallas kernels  69 us (99%)
    pallas_call x1, Pallas kernels, per_device(): pl.pallas_call(kernel, out_shape=(jax.ShapeDtypeStruct((OWN, WIDTH), BF16...  67.5 us
    pallas_call x1, Pallas kernels, per_device(): pl.pallas_call(hand_on, out_shape=(jax.ShapeDtypeStruct((OWN, WIDTH), BF1...  1.45 us

profile of v5, /device:TPU:1, one launch (start us, length us, event | category | flops | bytes accessed | tf_op | source)
XLA Modules:
  0.0 69.6 jit_solution(16603650746337768885)
XLA Ops:
  0.6 67.5 %shard_map.77 = (bf16[8,3584]{1,0:T(8,128)(2,1)}, f32[1,128]{1,0:T(1,128)}) custom-call(bf16[32,256]{1,0:T(8,128)(2,1)} %qa.1, bf16[8,3584]{1,0:T(8,128)(2,1)} %qg.1, f32[3,256,3584]{2,1,0:T(8,128)} %ritz.1, f32[3]{0:T(128)} %eig.1, bf16[8,8192]{1,0:T(8,128)(2,1)} %ta.1, bf16[8,3584]{1,0:T(8,128)(2,1)} %tg.1), custom_call_target="tpu_custom_call" | custom-call | tf_op jit(solution)/shard_map/pallas_call | solution.py:574
  68.1 1.5 %shard_map.78 = (bf16[8,3584]{1,0:T(8,128)(2,1)}, f32[1,8]{1,0:T(1,128)}) custom-call(bf16[8,3584]{1,0:T(8,128)(2,1)} %get-tuple-element.6.response, f32[1,128]{1,0:T(1,128)} %get-tuple-element.7.scores), custom_call_target="tpu_custom_call" | custom-call | tf_op jit(solution)/shard_map/pallas_call | solution.py:617

commit v6 on v5

--- a/solution.py
+++ b/solution.py
@@ -349,9 +349,10 @@
     acc = over_z(acc, at_y(2), 5, 8)
 
     line = lax.broadcasted_iota(jnp.int32, (8, 128), 0)
-    mine = jnp.zeros((8, 128), F32)
+    place = lax.broadcasted_iota(jnp.int32, (1, 128), 1)
+    mine = jnp.zeros((1, 128), F32)
     for k in range(RITZ):
-        mine = jnp.where(line == k, jnp.sum(acc[k], axis=0, keepdims=True), mine)
+        mine = jnp.where(place == k, jnp.sum(acc[k], axis=(0, 1), keepdims=True), mine)
     c_col[col] = mine
     spread(c_col.at[col], c_col.at[col], 2, "col", COLS)
     spread_done(c_col, 2, "col", COLS).wait_recv()
@@ -367,7 +368,7 @@
     total = jnp.sum(c_row[...], axis=0)
     weights = []
     for k in range(RITZ):
-        coeff = jnp.sum(jnp.where(line == k, total, 0.0), axis=(0, 1), keepdims=True)
+        coeff = jnp.sum(jnp.where(place == k, total, 0.0), axis=1, keepdims=True)
         scale = jnp.full((1, 1), eig[k], F32) * math.sqrt(QUERY * D_OUT)
         weights.append(jnp.broadcast_to(coeff / scale, (8, 128)))
 
@@ -599,8 +600,8 @@
             vmem((NZ, SY // 128 + 1, OWN, 128), BF16),
             vmem((NZ, SY // 128 + 1, OWN, 128), BF16),
             vmem((NZ * SY // 256, OWN, 128), F32),
-            vmem((COLS, 8, 128), F32),
-            vmem((ROWS, 8, 128), F32),
+            vmem((COLS, 1, 128), F32),
+            vmem((ROWS, 1, 128), F32),
             vmem((COLS, 8, 128), F32),
             dma((5 + WIDTH // CHUNK,)),
             dma((N_WIRE,)),

time: 69.7 us -> 67.4 us (0.967)
  Pallas kernels: 69 us -> 66.6 us
    pallas_call x1, Pallas kernels: 67.5 us -> 65.2 us  [per_device(): pl.pallas_call(kernel, out_shape=(jax.ShapeDtypeStruct((OWN, WIDTH), BF16...]
where the time goes in v6:
time: 67.4 us; the launch traced here: 67.3 us
  Pallas kernels  66.6 us (99%)
    pallas_call x1, Pallas kernels, per_device(): pl.pallas_call(kernel, out_shape=(jax.ShapeDtypeStruct((OWN, WIDTH), BF16...  65.2 us
    pallas_call x1, Pallas kernels, per_device(): pl.pallas_call(hand_on, out_shape=(jax.ShapeDtypeStruct((OWN, WIDTH), BF1...  1.45 us

profile of v6, /device:TPU:1, one launch (start us, length us, event | category | flops | bytes accessed | tf_op | source)
XLA Modules:
  0.0 67.3 jit_solution(6488054886415562000)
XLA Ops:
  0.6 65.2 %shard_map.77 = (bf16[8,3584]{1,0:T(8,128)(2,1)}, f32[1,128]{1,0:T(1,128)}) custom-call(bf16[32,256]{1,0:T(8,128)(2,1)} %qa.1, bf16[8,3584]{1,0:T(8,128)(2,1)} %qg.1, f32[3,256,3584]{2,1,0:T(8,128)} %ritz.1, f32[3]{0:T(128)} %eig.1, bf16[8,8192]{1,0:T(8,128)(2,1)} %ta.1, bf16[8,3584]{1,0:T(8,128)(2,1)} %tg.1), custom_call_target="tpu_custom_call" | custom-call | tf_op jit(solution)/shard_map/pallas_call | solution.py:575
  65.8 1.5 %shard_map.78 = (bf16[8,3584]{1,0:T(8,128)(2,1)}, f32[1,8]{1,0:T(1,128)}) custom-call(bf16[8,3584]{1,0:T(8,128)(2,1)} %get-tuple-element.6.response, f32[1,128]{1,0:T(1,128)} %get-tuple-element.7.scores), custom_call_target="tpu_custom_call" | custom-call | tf_op jit(solution)/shard_map/pallas_call | solution.py:618
